TPU v7x, 512 devices: a whole 4x8x8 slice. The times are simulated.
512 devices in a mesh: tm: 32 (over y, x), blk: 16 (over z, core).
Axes of the slice: x: 4, y: 8, z: 8, core: 2. Of those that a mesh axis runs over, the one named last changes fastest.
Arguments:
- panel_strip: bfloat16 [32, 8192, 2304], P('tm', 'blk'), may hold values from -6 to 6
- pivot_inverses: bfloat16 [32, 2, 256, 256], P('tm'), may hold values from -0.0234375 to 0.0234375
- coupling: float32 [32, 256, 256], P('tm'), may hold values from -0.375 to 0.375
- pivot_nodes: int32 [3, 256], replicated, may hold values from 0 to 8191, as said below
Outputs:
- trailing: bfloat16 [32, 8192, 1792], P('tm', 'blk')
- reduced: float32 [32, 256, 256], P('tm')
Inputs may be any that keep to these rules, and one draw needn't show every extreme that they name: `pivot_nodes`: entry j of every row is a node of the range [(j // 16) * 512, (j // 16 + 1) * 512); all 768 entries differ.
All inputs are finite; a program needn't handle non-finite values.
Results may differ from a plain program's by a relative error of at most 0.0068.
Values may be sent and summed in bfloat16 or wider, within the bound.
No kernel may reach another device: no remote copies, remote signals or barrier semaphores. Data moves between devices by JAX's collectives and lax.ppermute only.
A program may use at most 128 MiB of HBM per device.

v0:
```python
import jax
import jax.numpy as jnp
from jax import lax
from jax.sharding import PartitionSpec as P


def passed_along(x, axis, by):
    count = lax.axis_size(axis)
    pairs = [(i, i + by) for i in range(count) if 0 <= i + by < count]
    return lax.ppermute(x, axis, pairs)


def matmul_high(left, right):
    return jnp.dot(left, right, precision=lax.Precision.HIGHEST, preferred_element_type=jnp.float32)


def body(panel_strip, pivot_inverses, coupling, pivot_nodes):
    strip_block = panel_strip[0]
    inverse_pair = pivot_inverses[0]
    coupling_here = coupling[0]
    panel_width = inverse_pair.shape[-1]
    rows_here = strip_block.shape[0]
    blk_count = lax.axis_size("blk")
    per_device = panel_width // blk_count
    my_index = lax.axis_index("blk")
    local_rows = (
        lax.dynamic_slice_in_dim(pivot_nodes, my_index * per_device, per_device, 1)
        - my_index * rows_here
    )
    picker = (
        local_rows[:, :, None] == lax.broadcasted_iota(jnp.int32, (3, per_device, rows_here), 2)
    ).astype(jnp.bfloat16)
    factor_one = jnp.dot(
        strip_block[:, :panel_width], inverse_pair[0], preferred_element_type=jnp.float32
    ).astype(jnp.bfloat16)
    picked_one = jnp.dot(
        picker[0], strip_block[:, panel_width:], preferred_element_type=jnp.float32
    ).astype(jnp.bfloat16)
    columns = factor_one
    updated = (
        strip_block[:, panel_width:].astype(jnp.float32)
        - jnp.dot(
            columns,
            lax.all_gather(picked_one, "blk", axis=0, tiled=True),
            preferred_element_type=jnp.float32,
        )
    ).astype(jnp.bfloat16)
    factor_two = jnp.dot(
        updated[:, :panel_width], inverse_pair[1], preferred_element_type=jnp.float32
    ).astype(jnp.bfloat16)
    picked_two = jnp.dot(
        picker[1], updated[:, panel_width:], preferred_element_type=jnp.float32
    ).astype(jnp.bfloat16)
    columns = factor_two
    trailing = (
        updated[:, panel_width:].astype(jnp.float32)
        - jnp.dot(
            columns,
            lax.all_gather(picked_two, "blk", axis=0, tiled=True),
            preferred_element_type=jnp.float32,
        )
    ).astype(jnp.bfloat16)
    edge_rows = jnp.dot(
        picker[2], trailing[:, :panel_width], preferred_element_type=jnp.float32
    ).astype(jnp.bfloat16)
    boundary_block = lax.all_gather(edge_rows, "blk", axis=0, tiled=True).astype(jnp.float32)
    position = lax.axis_index("tm")

    def advance(turn_index, current):
        incoming = passed_along(current, "tm", 1)

        def apply_map(operand):
            return (
                matmul_high(matmul_high(coupling_here, operand), coupling_here.T) + boundary_block
            )

        def keep_state(operand):
            return current

        return lax.cond(position == turn_index, apply_map, keep_state, incoming)

    reduced = lax.fori_loop(1, lax.axis_size("tm"), advance, boundary_block)
    return (trailing[None], reduced[None])


def solution(mesh):
    placed = (P("tm", "blk", None), P("tm", None, None, None), P("tm", None, None), P())
    return jax.shard_map(
        body,
        mesh=mesh,
        in_specs=placed,
        out_specs=(P("tm", "blk", None), P("tm", None, None)),
        check_vma=False,
    )
```

profile of v0, /device:TPU:32, one launch (start us, length us, event | category | flops | bytes accessed | tf_op | source)
XLA Modules:
  0.0 484.5 jit_solution(10073837723274590851)
XLA Ops:
  8.1 2.6 convolution_convert_fusion.1
  10.7 46.4 %all-gather.2.cloned.1.call-done = bf16[256,2048]{1,0:T(8,128)(2,1)} async-done(((bf16[16,2048]{1,0:T(8,128)(2,1)}), bf16[256,2048]{1,0:T(8,128)(2,1)}) %all-gather.2.cloned.1.call-update) | async-done | bytes 1048592 | tf_op jit(solution)/shard_map/all_gather | solution.py:44
  57.1 2.8 subtract_convert_fusion
  60.3 18.0 %all_gather.10 = bf16[256,1792]{1,0:T(8,128)(2,1)S(1)} all-gather(bf16[16,1792]{1,0:T(8,128)(2,1)S(1)} %convolution_convert_fusion), channel_id=1, replica_groups=mesh['tm'=32,'blk'=16] {'blk'}, dimensions={0}, use_global_device_ids=true | all-gather | bytes 974848 | tf_op jit(solution)/shard_map/all_gather | solution.py:59
  78.3 3.0 subtract_convert_fusion.1
  82.4 15.1 %all_gather.11 = bf16[256,256]{1,0:T(8,128)(2,1)S(1)} all-gather(bf16[16,256]{1,0:T(8,128)(2,1)S(1)} %convolution_convert_fusion.4), channel_id=1, replica_groups=mesh['tm'=32,'blk'=16] {'blk'}, dimensions={0}, use_global_device_ids=true | all-gather | bytes 139264 | tf_op jit(solution)/shard_map/all_gather | solution.py:66
  97.6 379.3 %while.16 = (s32[]{:T(128)}, f32[256,256]{1,0:T(8,128)S(1)}, s32[]{:T(128)}, f32[256,256]{1,0:T(8,128)S(1)}, f32[256,256]{1,0:T(8,128)S(1)}, /*index=5*/s32[]{:T(128)}) while((s32[]{:T(128)}, f32[256,256]{1,0:T(8,128)S(1)}, s32[]{:T(128)}, f32[256,256]{1,0:T(8,128)S(1)}, f32[256,256]{1,0:T(8,128)S(1)}, /*index=5*/s32[]{:T(128)}) %tuple.51), condition=%wide.region_3.0_spmd, body=%wide.region_0.0_spmd.sunk | while | flops 402718720 | bytes 2883739 | solution.py:82
  97.6 3.4 collective-permute-start
  101.0 10.4 %collective-permute-done = f32[256,256]{1,0:T(8,128)S(1)} collective-permute-done((f32[256,256]{1,0:T(8,128)S(1)}, f32[256,256]{1,0:T(8,128)S(1)}, u32[]{:S(2)}, u32[]{:S(2)}) %collective-permute-start) | collective-permute-done | bytes 262176 | tf_op jit(solution)/shard_map/while/body/eval_jaxpr/ppermute | solution.py:10
  111.4 1.9 collective-permute-start
  113.3 11.0 %collective-permute-done = f32[256,256]{1,0:T(8,128)S(1)} collective-permute-done((f32[256,256]{1,0:T(8,128)S(1)}, f32[256,256]{1,0:T(8,128)S(1)}, u32[]{:S(2)}, u32[]{:S(2)}) %collective-permute-start) | collective-permute-done | bytes 262176 | tf_op jit(solution)/shard_map/while/body/eval_jaxpr/ppermute | solution.py:10
  124.3 1.9 collective-permute-start
  126.3 10.1 %collective-permute-done = f32[256,256]{1,0:T(8,128)S(1)} collective-permute-done((f32[256,256]{1,0:T(8,128)S(1)}, f32[256,256]{1,0:T(8,128)S(1)}, u32[]{:S(2)}, u32[]{:S(2)}) %collective-permute-start) | collective-permute-done | bytes 262176 | tf_op jit(solution)/shard_map/while/body/eval_jaxpr/ppermute | solution.py:10
  136.4 1.9 collective-permute-start
  138.3 9.7 %collective-permute-done = f32[256,256]{1,0:T(8,128)S(1)} collective-permute-done((f32[256,256]{1,0:T(8,128)S(1)}, f32[256,256]{1,0:T(8,128)S(1)}, u32[]{:S(2)}, u32[]{:S(2)}) %collective-permute-start) | collective-permute-done | bytes 262176 | tf_op jit(solution)/shard_map/while/body/eval_jaxpr/ppermute | solution.py:10
  147.9 1.9 collective-permute-start
  149.9 9.7 %collective-permute-done = f32[256,256]{1,0:T(8,128)S(1)} collective-permute-done((f32[256,256]{1,0:T(8,128)S(1)}, f32[256,256]{1,0:T(8,128)S(1)}, u32[]{:S(2)}, u32[]{:S(2)}) %collective-permute-start) | collective-permute-done | bytes 262176 | tf_op jit(solution)/shard_map/while/body/eval_jaxpr/ppermute | solution.py:10
  159.5 1.9 collective-permute-start
  161.4 9.7 %collective-permute-done = f32[256,256]{1,0:T(8,128)S(1)} collective-permute-done((f32[256,256]{1,0:T(8,128)S(1)}, f32[256,256]{1,0:T(8,128)S(1)}, u32[]{:S(2)}, u32[]{:S(2)}) %collective-permute-start) | collective-permute-done | bytes 262176 | tf_op jit(solution)/shard_map/while/body/eval_jaxpr/ppermute | solution.py:10
  171.1 1.9 collective-permute-start
  173.0 9.7 %collective-permute-done = f32[256,256]{1,0:T(8,128)S(1)} collective-permute-done((f32[256,256]{1,0:T(8,128)S(1)}, f32[256,256]{1,0:T(8,128)S(1)}, u32[]{:S(2)}, u32[]{:S(2)}) %collective-permute-start) | collective-permute-done | bytes 262176 | tf_op jit(solution)/shard_map/while/body/eval_jaxpr/ppermute | solution.py:10
  182.7 1.9 collective-permute-start
  184.6 9.8 %collective-permute-done = f32[256,256]{1,0:T(8,128)S(1)} collective-permute-done((f32[256,256]{1,0:T(8,128)S(1)}, f32[256,256]{1,0:T(8,128)S(1)}, u32[]{:S(2)}, u32[]{:S(2)}) %collective-permute-start) | collective-permute-done | bytes 262176 | tf_op jit(solution)/shard_map/while/body/eval_jaxpr/ppermute | solution.py:10
  194.4 1.9 collective-permute-start
  196.3 10.9 %collective-permute-done = f32[256,256]{1,0:T(8,128)S(1)} collective-permute-done((f32[256,256]{1,0:T(8,128)S(1)}, f32[256,256]{1,0:T(8,128)S(1)}, u32[]{:S(2)}, u32[]{:S(2)}) %collective-permute-start) | collective-permute-done | bytes 262176 | tf_op jit(solution)/shard_map/while/body/eval_jaxpr/ppermute | solution.py:10
  207.3 1.9 collective-permute-start
  209.2 12.1 %collective-permute-done = f32[256,256]{1,0:T(8,128)S(1)} collective-permute-done((f32[256,256]{1,0:T(8,128)S(1)}, f32[256,256]{1,0:T(8,128)S(1)}, u32[]{:S(2)}, u32[]{:S(2)}) %collective-permute-start) | collective-permute-done | bytes 262176 | tf_op jit(solution)/shard_map/while/body/eval_jaxpr/ppermute | solution.py:10
  221.3 1.9 collective-permute-start
  223.3 11.6 %collective-permute-done = f32[256,256]{1,0:T(8,128)S(1)} collective-permute-done((f32[256,256]{1,0:T(8,128)S(1)}, f32[256,256]{1,0:T(8,128)S(1)}, u32[]{:S(2)}, u32[]{:S(2)}) %collective-permute-start) | collective-permute-done | bytes 262176 | tf_op jit(solution)/shard_map/while/body/eval_jaxpr/ppermute | solution.py:10
  234.9 1.9 collective-permute-start
  236.8 10.8 %collective-permute-done = f32[256,256]{1,0:T(8,128)S(1)} collective-permute-done((f32[256,256]{1,0:T(8,128)S(1)}, f32[256,256]{1,0:T(8,128)S(1)}, u32[]{:S(2)}, u32[]{:S(2)}) %collective-permute-start) | collective-permute-done | bytes 262176 | tf_op jit(solution)/shard_map/while/body/eval_jaxpr/ppermute | solution.py:10
  247.6 1.9 collective-permute-start
  249.5 9.9 %collective-permute-done = f32[256,256]{1,0:T(8,128)S(1)} collective-permute-done((f32[256,256]{1,0:T(8,128)S(1)}, f32[256,256]{1,0:T(8,128)S(1)}, u32[]{:S(2)}, u32[]{:S(2)}) %collective-permute-start) | collective-permute-done | bytes 262176 | tf_op jit(solution)/shard_map/while/body/eval_jaxpr/ppermute | solution.py:10
  259.4 1.9 collective-permute-start
  261.3 9.7 %collective-permute-done = f32[256,256]{1,0:T(8,128)S(1)} collective-permute-done((f32[256,256]{1,0:T(8,128)S(1)}, f32[256,256]{1,0:T(8,128)S(1)}, u32[]{:S(2)}, u32[]{:S(2)}) %collective-permute-start) | collective-permute-done | bytes 262176 | tf_op jit(solution)/shard_map/while/body/eval_jaxpr/ppermute | solution.py:10
  271.0 1.9 collective-permute-start
  272.9 9.7 %collective-permute-done = f32[256,256]{1,0:T(8,128)S(1)} collective-permute-done((f32[256,256]{1,0:T(8,128)S(1)}, f32[256,256]{1,0:T(8,128)S(1)}, u32[]{:S(2)}, u32[]{:S(2)}) %collective-permute-start) | collective-permute-done | bytes 262176 | tf_op jit(solution)/shard_map/while/body/eval_jaxpr/ppermute | solution.py:10
  282.5 1.9 collective-permute-start
  284.5 9.7 %collective-permute-done = f32[256,256]{1,0:T(8,128)S(1)} collective-permute-done((f32[256,256]{1,0:T(8,128)S(1)}, f32[256,256]{1,0:T(8,128)S(1)}, u32[]{:S(2)}, u32[]{:S(2)}) %collective-permute-start) | collective-permute-done | bytes 262176 | tf_op jit(solution)/shard_map/while/body/eval_jaxpr/ppermute | solution.py:10
  294.9 1.9 collective-permute-start
  296.9 9.7 %collective-permute-done = f32[256,256]{1,0:T(8,128)S(1)} collective-permute-done((f32[256,256]{1,0:T(8,128)S(1)}, f32[256,256]{1,0:T(8,128)S(1)}, u32[]{:S(2)}, u32[]{:S(2)}) %collective-permute-start) | collective-permute-done | bytes 262176 | tf_op jit(solution)/shard_map/while/body/eval_jaxpr/ppermute | solution.py:10
  306.5 1.9 collective-permute-start
  308.4 10.1 %collective-permute-done = f32[256,256]{1,0:T(8,128)S(1)} collective-permute-done((f32[256,256]{1,0:T(8,128)S(1)}, f32[256,256]{1,0:T(8,128)S(1)}, u32[]{:S(2)}, u32[]{:S(2)}) %collective-permute-start) | collective-permute-done | bytes 262176 | tf_op jit(solution)/shard_map/while/body/eval_jaxpr/ppermute | solution.py:10
  318.5 1.9 collective-permute-start
  320.4 11.2 %collective-permute-done = f32[256,256]{1,0:T(8,128)S(1)} collective-permute-done((f32[256,256]{1,0:T(8,128)S(1)}, f32[256,256]{1,0:T(8,128)S(1)}, u32[]{:S(2)}, u32[]{:S(2)}) %collective-permute-start) | collective-permute-done | bytes 262176 | tf_op jit(solution)/shard_map/while/body/eval_jaxpr/ppermute | solution.py:10
  331.6 1.9 collective-permute-start
  333.6 12.3 %collective-permute-done = f32[256,256]{1,0:T(8,128)S(1)} collective-permute-done((f32[256,256]{1,0:T(8,128)S(1)}, f32[256,256]{1,0:T(8,128)S(1)}, u32[]{:S(2)}, u32[]{:S(2)}) %collective-permute-start) | collective-permute-done | bytes 262176 | tf_op jit(solution)/shard_map/while/body/eval_jaxpr/ppermute | solution.py:10
  345.9 1.9 collective-permute-start
  347.8 11.6 %collective-permute-done = f32[256,256]{1,0:T(8,128)S(1)} collective-permute-done((f32[256,256]{1,0:T(8,128)S(1)}, f32[256,256]{1,0:T(8,128)S(1)}, u32[]{:S(2)}, u32[]{:S(2)}) %collective-permute-start) | collective-permute-done | bytes 262176 | tf_op jit(solution)/shard_map/while/body/eval_jaxpr/ppermute | solution.py:10
  359.4 1.9 collective-permute-start
  361.3 10.8 %collective-permute-done = f32[256,256]{1,0:T(8,128)S(1)} collective-permute-done((f32[256,256]{1,0:T(8,128)S(1)}, f32[256,256]{1,0:T(8,128)S(1)}, u32[]{:S(2)}, u32[]{:S(2)}) %collective-permute-start) | collective-permute-done | bytes 262176 | tf_op jit(solution)/shard_map/while/body/eval_jaxpr/ppermute | solution.py:10
  372.1 1.9 collective-permute-start
  374.0 9.8 %collective-permute-done = f32[256,256]{1,0:T(8,128)S(1)} collective-permute-done((f32[256,256]{1,0:T(8,128)S(1)}, f32[256,256]{1,0:T(8,128)S(1)}, u32[]{:S(2)}, u32[]{:S(2)}) %collective-permute-start) | collective-permute-done | bytes 262176 | tf_op jit(solution)/shard_map/while/body/eval_jaxpr/ppermute | solution.py:10
  383.9 1.9 collective-permute-start
  385.8 9.7 %collective-permute-done = f32[256,256]{1,0:T(8,128)S(1)} collective-permute-done((f32[256,256]{1,0:T(8,128)S(1)}, f32[256,256]{1,0:T(8,128)S(1)}, u32[]{:S(2)}, u32[]{:S(2)}) %collective-permute-start) | collective-permute-done | bytes 262176 | tf_op jit(solution)/shard_map/while/body/eval_jaxpr/ppermute | solution.py:10
  395.5 1.9 collective-permute-start
  397.4 9.7 %collective-permute-done = f32[256,256]{1,0:T(8,128)S(1)} collective-permute-done((f32[256,256]{1,0:T(8,128)S(1)}, f32[256,256]{1,0:T(8,128)S(1)}, u32[]{:S(2)}, u32[]{:S(2)}) %collective-permute-start) | collective-permute-done | bytes 262176 | tf_op jit(solution)/shard_map/while/body/eval_jaxpr/ppermute | solution.py:10
  407.0 1.9 collective-permute-start
  409.0 9.7 %collective-permute-done = f32[256,256]{1,0:T(8,128)S(1)} collective-permute-done((f32[256,256]{1,0:T(8,128)S(1)}, f32[256,256]{1,0:T(8,128)S(1)}, u32[]{:S(2)}, u32[]{:S(2)}) %collective-permute-start) | collective-permute-done | bytes 262176 | tf_op jit(solution)/shard_map/while/body/eval_jaxpr/ppermute | solution.py:10
  420.5 9.7 %collective-permute-done = f32[256,256]{1,0:T(8,128)S(1)} collective-permute-done((f32[256,256]{1,0:T(8,128)S(1)}, f32[256,256]{1,0:T(8,128)S(1)}, u32[]{:S(2)}, u32[]{:S(2)}) %collective-permute-start) | collective-permute-done | bytes 262176 | tf_op jit(solution)/shard_map/while/body/eval_jaxpr/ppermute | solution.py:10
  432.1 10.1 %collective-permute-done = f32[256,256]{1,0:T(8,128)S(1)} collective-permute-done((f32[256,256]{1,0:T(8,128)S(1)}, f32[256,256]{1,0:T(8,128)S(1)}, u32[]{:S(2)}, u32[]{:S(2)}) %collective-permute-start) | collective-permute-done | bytes 262176 | tf_op jit(solution)/shard_map/while/body/eval_jaxpr/ppermute | solution.py:10
  444.1 9.7 %collective-permute-done = f32[256,256]{1,0:T(8,128)S(1)} collective-permute-done((f32[256,256]{1,0:T(8,128)S(1)}, f32[256,256]{1,0:T(8,128)S(1)}, u32[]{:S(2)}, u32[]{:S(2)}) %collective-permute-start) | collective-permute-done | bytes 262176 | tf_op jit(solution)/shard_map/while/body/eval_jaxpr/ppermute | solution.py:10
  455.7 9.7 %collective-permute-done = f32[256,256]{1,0:T(8,128)S(1)} collective-permute-done((f32[256,256]{1,0:T(8,128)S(1)}, f32[256,256]{1,0:T(8,128)S(1)}, u32[]{:S(2)}, u32[]{:S(2)}) %collective-permute-start) | collective-permute-done | bytes 262176 | tf_op jit(solution)/shard_map/while/body/eval_jaxpr/ppermute | solution.py:10
  467.3 9.7 %collective-permute-done = f32[256,256]{1,0:T(8,128)S(1)} collective-permute-done((f32[256,256]{1,0:T(8,128)S(1)}, f32[256,256]{1,0:T(8,128)S(1)}, u32[]{:S(2)}, u32[]{:S(2)}) %collective-permute-start) | collective-permute-done | bytes 262176 | tf_op jit(solution)/shard_map/while/body/eval_jaxpr/ppermute | solution.py:10
  (52 shorter events, 14.3 us)
Async XLA Ops:
  7.2 50.0 %copy-start.2 = (bf16[1,2,256,256]{3,2,1,0:T(8,128)(2,1)S(1)}, bf16[1,2,256,256]{3,2,1,0:T(8,128)(2,1)}, u32[]{:S(2)}) copy-start(bf16[1,2,256,256]{3,2,1,0:T(8,128)(2,1)} %param.9) | copy-start | bytes 786436
  7.2 50.0 %all-gather.2.cloned.1.call-start = ((), (), s32[]{:S(2)}) async-start(), calls=%async_computation | async-start | bytes 1114112 | tf_op jit(solution)/shard_map/all_gather | solution.py:44
  78.3 19.3 %copy-start = (f32[1,256,256]{2,1,0:T(8,128)S(1)}, f32[1,256,256]{2,1,0:T(8,128)}, u32[]{:S(2)}) copy-start(f32[1,256,256]{2,1,0:T(8,128)} %param.10) | copy-start | bytes 786436
  97.6 13.8 %collective-permute-start = (f32[256,256]{1,0:T(8,128)S(1)}, f32[256,256]{1,0:T(8,128)S(1)}, u32[]{:S(2)}, u32[]{:S(2)}) collective-permute-start(f32[256,256]{1,0:T(8,128)S(1)} %get-tuple-element.162), channel_id=1, source_target_pairs={{0,16},{16,32},{32,48},{48,64},{64,80},{80,96},{96,112},{112,128},... | collective-permute-start | bytes 786440 | tf_op jit(solution)/shard_map/while/body/eval_jaxpr/ppermute | solution.py:10
  111.4 13.0 %collective-permute-start = (f32[256,256]{1,0:T(8,128)S(1)}, f32[256,256]{1,0:T(8,128)S(1)}, u32[]{:S(2)}, u32[]{:S(2)}) collective-permute-start(f32[256,256]{1,0:T(8,128)S(1)} %get-tuple-element.162), channel_id=1, source_target_pairs={{0,16},{16,32},{32,48},{48,64},{64,80},{80,96},{96,112},{112,128},... | collective-permute-start | bytes 786440 | tf_op jit(solution)/shard_map/while/body/eval_jaxpr/ppermute | solution.py:10
  124.3 12.0 %collective-permute-start = (f32[256,256]{1,0:T(8,128)S(1)}, f32[256,256]{1,0:T(8,128)S(1)}, u32[]{:S(2)}, u32[]{:S(2)}) collective-permute-start(f32[256,256]{1,0:T(8,128)S(1)} %get-tuple-element.162), channel_id=1, source_target_pairs={{0,16},{16,32},{32,48},{48,64},{64,80},{80,96},{96,112},{112,128},... | collective-permute-start | bytes 786440 | tf_op jit(solution)/shard_map/while/body/eval_jaxpr/ppermute | solution.py:10
  136.4 11.6 %collective-permute-start = (f32[256,256]{1,0:T(8,128)S(1)}, f32[256,256]{1,0:T(8,128)S(1)}, u32[]{:S(2)}, u32[]{:S(2)}) collective-permute-start(f32[256,256]{1,0:T(8,128)S(1)} %get-tuple-element.162), channel_id=1, source_target_pairs={{0,16},{16,32},{32,48},{48,64},{64,80},{80,96},{96,112},{112,128},... | collective-permute-start | bytes 786440 | tf_op jit(solution)/shard_map/while/body/eval_jaxpr/ppermute | solution.py:10
  147.9 11.6 %collective-permute-start = (f32[256,256]{1,0:T(8,128)S(1)}, f32[256,256]{1,0:T(8,128)S(1)}, u32[]{:S(2)}, u32[]{:S(2)}) collective-permute-start(f32[256,256]{1,0:T(8,128)S(1)} %get-tuple-element.162), channel_id=1, source_target_pairs={{0,16},{16,32},{32,48},{48,64},{64,80},{80,96},{96,112},{112,128},... | collective-permute-start | bytes 786440 | tf_op jit(solution)/shard_map/while/body/eval_jaxpr/ppermute | solution.py:10
  159.5 11.6 %collective-permute-start = (f32[256,256]{1,0:T(8,128)S(1)}, f32[256,256]{1,0:T(8,128)S(1)}, u32[]{:S(2)}, u32[]{:S(2)}) collective-permute-start(f32[256,256]{1,0:T(8,128)S(1)} %get-tuple-element.162), channel_id=1, source_target_pairs={{0,16},{16,32},{32,48},{48,64},{64,80},{80,96},{96,112},{112,128},... | collective-permute-start | bytes 786440 | tf_op jit(solution)/shard_map/while/body/eval_jaxpr/ppermute | solution.py:10
  171.1 11.6 %collective-permute-start = (f32[256,256]{1,0:T(8,128)S(1)}, f32[256,256]{1,0:T(8,128)S(1)}, u32[]{:S(2)}, u32[]{:S(2)}) collective-permute-start(f32[256,256]{1,0:T(8,128)S(1)} %get-tuple-element.162), channel_id=1, source_target_pairs={{0,16},{16,32},{32,48},{48,64},{64,80},{80,96},{96,112},{112,128},... | collective-permute-start | bytes 786440 | tf_op jit(solution)/shard_map/while/body/eval_jaxpr/ppermute | solution.py:10
  182.7 11.8 %collective-permute-start = (f32[256,256]{1,0:T(8,128)S(1)}, f32[256,256]{1,0:T(8,128)S(1)}, u32[]{:S(2)}, u32[]{:S(2)}) collective-permute-start(f32[256,256]{1,0:T(8,128)S(1)} %get-tuple-element.162), channel_id=1, source_target_pairs={{0,16},{16,32},{32,48},{48,64},{64,80},{80,96},{96,112},{112,128},... | collective-permute-start | bytes 786440 | tf_op jit(solution)/shard_map/while/body/eval_jaxpr/ppermute | solution.py:10
  194.4 12.8 %collective-permute-start = (f32[256,256]{1,0:T(8,128)S(1)}, f32[256,256]{1,0:T(8,128)S(1)}, u32[]{:S(2)}, u32[]{:S(2)}) collective-permute-start(f32[256,256]{1,0:T(8,128)S(1)} %get-tuple-element.162), channel_id=1, source_target_pairs={{0,16},{16,32},{32,48},{48,64},{64,80},{80,96},{96,112},{112,128},... | collective-permute-start | bytes 786440 | tf_op jit(solution)/shard_map/while/body/eval_jaxpr/ppermute | solution.py:10
  207.3 14.1 %collective-permute-start = (f32[256,256]{1,0:T(8,128)S(1)}, f32[256,256]{1,0:T(8,128)S(1)}, u32[]{:S(2)}, u32[]{:S(2)}) collective-permute-start(f32[256,256]{1,0:T(8,128)S(1)} %get-tuple-element.162), channel_id=1, source_target_pairs={{0,16},{16,32},{32,48},{48,64},{64,80},{80,96},{96,112},{112,128},... | collective-permute-start | bytes 786440 | tf_op jit(solution)/shard_map/while/body/eval_jaxpr/ppermute | solution.py:10
  221.3 13.5 %collective-permute-start = (f32[256,256]{1,0:T(8,128)S(1)}, f32[256,256]{1,0:T(8,128)S(1)}, u32[]{:S(2)}, u32[]{:S(2)}) collective-permute-start(f32[256,256]{1,0:T(8,128)S(1)} %get-tuple-element.162), channel_id=1, source_target_pairs={{0,16},{16,32},{32,48},{48,64},{64,80},{80,96},{96,112},{112,128},... | collective-permute-start | bytes 786440 | tf_op jit(solution)/shard_map/while/body/eval_jaxpr/ppermute | solution.py:10
  234.9 12.7 %collective-permute-start = (f32[256,256]{1,0:T(8,128)S(1)}, f32[256,256]{1,0:T(8,128)S(1)}, u32[]{:S(2)}, u32[]{:S(2)}) collective-permute-start(f32[256,256]{1,0:T(8,128)S(1)} %get-tuple-element.162), channel_id=1, source_target_pairs={{0,16},{16,32},{32,48},{48,64},{64,80},{80,96},{96,112},{112,128},... | collective-permute-start | bytes 786440 | tf_op jit(solution)/shard_map/while/body/eval_jaxpr/ppermute | solution.py:10
  247.6 11.8 %collective-permute-start = (f32[256,256]{1,0:T(8,128)S(1)}, f32[256,256]{1,0:T(8,128)S(1)}, u32[]{:S(2)}, u32[]{:S(2)}) collective-permute-start(f32[256,256]{1,0:T(8,128)S(1)} %get-tuple-element.162), channel_id=1, source_target_pairs={{0,16},{16,32},{32,48},{48,64},{64,80},{80,96},{96,112},{112,128},... | collective-permute-start | bytes 786440 | tf_op jit(solution)/shard_map/while/body/eval_jaxpr/ppermute | solution.py:10
  259.4 11.6 %collective-permute-start = (f32[256,256]{1,0:T(8,128)S(1)}, f32[256,256]{1,0:T(8,128)S(1)}, u32[]{:S(2)}, u32[]{:S(2)}) collective-permute-start(f32[256,256]{1,0:T(8,128)S(1)} %get-tuple-element.162), channel_id=1, source_target_pairs={{0,16},{16,32},{32,48},{48,64},{64,80},{80,96},{96,112},{112,128},... | collective-permute-start | bytes 786440 | tf_op jit(solution)/shard_map/while/body/eval_jaxpr/ppermute | solution.py:10
  271.0 11.6 %collective-permute-start = (f32[256,256]{1,0:T(8,128)S(1)}, f32[256,256]{1,0:T(8,128)S(1)}, u32[]{:S(2)}, u32[]{:S(2)}) collective-permute-start(f32[256,256]{1,0:T(8,128)S(1)} %get-tuple-element.162), channel_id=1, source_target_pairs={{0,16},{16,32},{32,48},{48,64},{64,80},{80,96},{96,112},{112,128},... | collective-permute-start | bytes 786440 | tf_op jit(solution)/shard_map/while/body/eval_jaxpr/ppermute | solution.py:10
  282.5 11.6 %collective-permute-start = (f32[256,256]{1,0:T(8,128)S(1)}, f32[256,256]{1,0:T(8,128)S(1)}, u32[]{:S(2)}, u32[]{:S(2)}) collective-permute-start(f32[256,256]{1,0:T(8,128)S(1)} %get-tuple-element.162), channel_id=1, source_target_pairs={{0,16},{16,32},{32,48},{48,64},{64,80},{80,96},{96,112},{112,128},... | collective-permute-start | bytes 786440 | tf_op jit(solution)/shard_map/while/body/eval_jaxpr/ppermute | solution.py:10
  294.9 11.6 %collective-permute-start = (f32[256,256]{1,0:T(8,128)S(1)}, f32[256,256]{1,0:T(8,128)S(1)}, u32[]{:S(2)}, u32[]{:S(2)}) collective-permute-start(f32[256,256]{1,0:T(8,128)S(1)} %get-tuple-element.162), channel_id=1, source_target_pairs={{0,16},{16,32},{32,48},{48,64},{64,80},{80,96},{96,112},{112,128},... | collective-permute-start | bytes 786440 | tf_op jit(solution)/shard_map/while/body/eval_jaxpr/ppermute | solution.py:10
  306.5 12.0 %collective-permute-start = (f32[256,256]{1,0:T(8,128)S(1)}, f32[256,256]{1,0:T(8,128)S(1)}, u32[]{:S(2)}, u32[]{:S(2)}) collective-permute-start(f32[256,256]{1,0:T(8,128)S(1)} %get-tuple-element.162), channel_id=1, source_target_pairs={{0,16},{16,32},{32,48},{48,64},{64,80},{80,96},{96,112},{112,128},... | collective-permute-start | bytes 786440 | tf_op jit(solution)/shard_map/while/body/eval_jaxpr/ppermute | solution.py:10
  318.5 13.1 %collective-permute-start = (f32[256,256]{1,0:T(8,128)S(1)}, f32[256,256]{1,0:T(8,128)S(1)}, u32[]{:S(2)}, u32[]{:S(2)}) collective-permute-start(f32[256,256]{1,0:T(8,128)S(1)} %get-tuple-element.162), channel_id=1, source_target_pairs={{0,16},{16,32},{32,48},{48,64},{64,80},{80,96},{96,112},{112,128},... | collective-permute-start | bytes 786440 | tf_op jit(solution)/shard_map/while/body/eval_jaxpr/ppermute | solution.py:10
  331.6 14.3 %collective-permute-start = (f32[256,256]{1,0:T(8,128)S(1)}, f32[256,256]{1,0:T(8,128)S(1)}, u32[]{:S(2)}, u32[]{:S(2)}) collective-permute-start(f32[256,256]{1,0:T(8,128)S(1)} %get-tuple-element.162), channel_id=1, source_target_pairs={{0,16},{16,32},{32,48},{48,64},{64,80},{80,96},{96,112},{112,128},... | collective-permute-start | bytes 786440 | tf_op jit(solution)/shard_map/while/body/eval_jaxpr/ppermute | solution.py:10
  345.9 13.5 %collective-permute-start = (f32[256,256]{1,0:T(8,128)S(1)}, f32[256,256]{1,0:T(8,128)S(1)}, u32[]{:S(2)}, u32[]{:S(2)}) collective-permute-start(f32[256,256]{1,0:T(8,128)S(1)} %get-tuple-element.162), channel_id=1, source_target_pairs={{0,16},{16,32},{32,48},{48,64},{64,80},{80,96},{96,112},{112,128},... | collective-permute-start | bytes 786440 | tf_op jit(solution)/shard_map/while/body/eval_jaxpr/ppermute | solution.py:10
  359.4 12.7 %collective-permute-start = (f32[256,256]{1,0:T(8,128)S(1)}, f32[256,256]{1,0:T(8,128)S(1)}, u32[]{:S(2)}, u32[]{:S(2)}) collective-permute-start(f32[256,256]{1,0:T(8,128)S(1)} %get-tuple-element.162), channel_id=1, source_target_pairs={{0,16},{16,32},{32,48},{48,64},{64,80},{80,96},{96,112},{112,128},... | collective-permute-start | bytes 786440 | tf_op jit(solution)/shard_map/while/body/eval_jaxpr/ppermute | solution.py:10
  372.1 11.8 %collective-permute-start = (f32[256,256]{1,0:T(8,128)S(1)}, f32[256,256]{1,0:T(8,128)S(1)}, u32[]{:S(2)}, u32[]{:S(2)}) collective-permute-start(f32[256,256]{1,0:T(8,128)S(1)} %get-tuple-element.162), channel_id=1, source_target_pairs={{0,16},{16,32},{32,48},{48,64},{64,80},{80,96},{96,112},{112,128},... | collective-permute-start | bytes 786440 | tf_op jit(solution)/shard_map/while/body/eval_jaxpr/ppermute | solution.py:10
  383.9 11.6 %collective-permute-start = (f32[256,256]{1,0:T(8,128)S(1)}, f32[256,256]{1,0:T(8,128)S(1)}, u32[]{:S(2)}, u32[]{:S(2)}) collective-permute-start(f32[256,256]{1,0:T(8,128)S(1)} %get-tuple-element.162), channel_id=1, source_target_pairs={{0,16},{16,32},{32,48},{48,64},{64,80},{80,96},{96,112},{112,128},... | collective-permute-start | bytes 786440 | tf_op jit(solution)/shard_map/while/body/eval_jaxpr/ppermute | solution.py:10
  395.5 11.6 %collective-permute-start = (f32[256,256]{1,0:T(8,128)S(1)}, f32[256,256]{1,0:T(8,128)S(1)}, u32[]{:S(2)}, u32[]{:S(2)}) collective-permute-start(f32[256,256]{1,0:T(8,128)S(1)} %get-tuple-element.162), channel_id=1, source_target_pairs={{0,16},{16,32},{32,48},{48,64},{64,80},{80,96},{96,112},{112,128},... | collective-permute-start | bytes 786440 | tf_op jit(solution)/shard_map/while/body/eval_jaxpr/ppermute | solution.py:10
  407.0 11.6 %collective-permute-start = (f32[256,256]{1,0:T(8,128)S(1)}, f32[256,256]{1,0:T(8,128)S(1)}, u32[]{:S(2)}, u32[]{:S(2)}) collective-permute-start(f32[256,256]{1,0:T(8,128)S(1)} %get-tuple-element.162), channel_id=1, source_target_pairs={{0,16},{16,32},{32,48},{48,64},{64,80},{80,96},{96,112},{112,128},... | collective-permute-start | bytes 786440 | tf_op jit(solution)/shard_map/while/body/eval_jaxpr/ppermute | solution.py:10
  418.6 11.6 %collective-permute-start = (f32[256,256]{1,0:T(8,128)S(1)}, f32[256,256]{1,0:T(8,128)S(1)}, u32[]{:S(2)}, u32[]{:S(2)}) collective-permute-start(f32[256,256]{1,0:T(8,128)S(1)} %get-tuple-element.162), channel_id=1, source_target_pairs={{0,16},{16,32},{32,48},{48,64},{64,80},{80,96},{96,112},{112,128},... | collective-permute-start | bytes 786440 | tf_op jit(solution)/shard_map/while/body/eval_jaxpr/ppermute | solution.py:10
  430.2 12.0 %collective-permute-start = (f32[256,256]{1,0:T(8,128)S(1)}, f32[256,256]{1,0:T(8,128)S(1)}, u32[]{:S(2)}, u32[]{:S(2)}) collective-permute-start(f32[256,256]{1,0:T(8,128)S(1)} %get-tuple-element.162), channel_id=1, source_target_pairs={{0,16},{16,32},{32,48},{48,64},{64,80},{80,96},{96,112},{112,128},... | collective-permute-start | bytes 786440 | tf_op jit(solution)/shard_map/while/body/eval_jaxpr/ppermute | solution.py:10
  442.2 11.6 %collective-permute-start = (f32[256,256]{1,0:T(8,128)S(1)}, f32[256,256]{1,0:T(8,128)S(1)}, u32[]{:S(2)}, u32[]{:S(2)}) collective-permute-start(f32[256,256]{1,0:T(8,128)S(1)} %get-tuple-element.162), channel_id=1, source_target_pairs={{0,16},{16,32},{32,48},{48,64},{64,80},{80,96},{96,112},{112,128},... | collective-permute-start | bytes 786440 | tf_op jit(solution)/shard_map/while/body/eval_jaxpr/ppermute | solution.py:10
  453.8 11.6 %collective-permute-start = (f32[256,256]{1,0:T(8,128)S(1)}, f32[256,256]{1,0:T(8,128)S(1)}, u32[]{:S(2)}, u32[]{:S(2)}) collective-permute-start(f32[256,256]{1,0:T(8,128)S(1)} %get-tuple-element.162), channel_id=1, source_target_pairs={{0,16},{16,32},{32,48},{48,64},{64,80},{80,96},{96,112},{112,128},... | collective-permute-start | bytes 786440 | tf_op jit(solution)/shard_map/while/body/eval_jaxpr/ppermute | solution.py:10
  465.4 11.6 %collective-permute-start = (f32[256,256]{1,0:T(8,128)S(1)}, f32[256,256]{1,0:T(8,128)S(1)}, u32[]{:S(2)}, u32[]{:S(2)}) collective-permute-start(f32[256,256]{1,0:T(8,128)S(1)} %get-tuple-element.162), channel_id=1, source_target_pairs={{0,16},{16,32},{32,48},{48,64},{64,80},{80,96},{96,112},{112,128},... | collective-permute-start | bytes 786440 | tf_op jit(solution)/shard_map/while/body/eval_jaxpr/ppermute | solution.py:10
  476.9 0.7 copy-start.1
Sparse Core Ops, SparseCore 0:
  10.9 46.2 all-gather.1
where the time goes:
time: 486 us; the launch traced here: 484 us
  waiting for transfers between devices  364 us (75%)
  starting transfers between devices  60.7 us (12%)
  blocking collectives  33.1 us (7%)
  between operations  14.1 us (3%)
  matrix products  10.7 us (2%)
    ppermute x31, waiting for transfers between devices, passed_along(): return lax.ppermute(x, axis, pairs)  317 us
    ppermute x31, starting transfers between devices, passed_along(): return lax.ppermute(x, axis, pairs)  60.6 us
    all_gather x1, waiting for transfers between devices, body(): lax.all_gather(picked_one, 'blk', axis=0, tiled=True)  46.4 us
    all_gather x1, blocking collectives, body(): lax.all_gather(picked_two, 'blk', axis=0, tiled=True)  18 us
    all_gather x1, blocking collectives, body(): lax.all_gather(edge_rows, 'blk', axis=0, tiled=True).astype(jnp.float32)  15.1 us
  transfers between devices with their start and end apart: 32, of which 32 were waited for; matrix products, arithmetic and copies ran while one was open for 0% of the time, Pallas kernels for 0%

commit v1 on v0

--- a/solution.py
+++ b/solution.py
@@ -2,6 +2,24 @@
 import jax.numpy as jnp
 from jax import lax
 from jax.sharding import PartitionSpec as P
+
+
+def collect(shard, axis, dim):
+    ways, here, hop = (lax.axis_size(axis), lax.axis_index(axis), shard.shape[dim])
+    shape = [n * ways if d == dim else n for d, n in enumerate(shard.shape)]
+    full = lax.dynamic_update_slice_in_dim(
+        jnp.zeros(shape, shard.dtype), shard, here * hop, axis=dim
+    )
+    going_up = going_down = shard
+    for far in range(1, ways // 2 + 1):
+        going_up = lax.ppermute(going_up, axis, [(d, (d + 1) % ways) for d in range(ways)])
+        full = lax.dynamic_update_slice_in_dim(full, going_up, (here - far) % ways * hop, axis=dim)
+        if 2 * far < ways:
+            going_down = lax.ppermute(going_down, axis, [(d, (d - 1) % ways) for d in range(ways)])
+            full = lax.dynamic_update_slice_in_dim(
+                full, going_down, (here + far) % ways * hop, axis=dim
+            )
+    return full
 
 
 def passed_along(x, axis, by):
@@ -54,11 +72,7 @@
     columns = factor_two
     trailing = (
         updated[:, panel_width:].astype(jnp.float32)
-        - jnp.dot(
-            columns,
-            lax.all_gather(picked_two, "blk", axis=0, tiled=True),
-            preferred_element_type=jnp.float32,
-        )
+        - jnp.dot(columns, collect(picked_two, "blk", 0), preferred_element_type=jnp.float32)
     ).astype(jnp.bfloat16)
     edge_rows = jnp.dot(
         picker[2], trailing[:, :panel_width], preferred_element_type=jnp.float32

time: 486 us -> 506 us (1.041)
  starting transfers between devices: 60.7 us -> 81.4 us
  blocking collectives: 33.1 us -> 14.5 us
  waiting for transfers between devices: 364 us -> 381 us
    ppermute x0 -> x15, starting transfers between devices: none -> 20.7 us  [the longest x7 20.4 us: collect(): lax.ppermute(going_down, axis, [(d, (d - 1) % ways) for d in range(ways)])]
    all_gather x1 -> x0, blocking collectives: 18 us -> none  [body(): lax.all_gather(picked_two, 'blk', axis=0, tiled=True)]
    ppermute x0 -> x15, waiting for transfers between devices: none -> 17.6 us  [the longest x8 17.6 us: collect(): lax.ppermute(going_up, axis, [(d, (d + 1) % ways) for d in range(ways)])]
  transfers between devices with their start and end apart: 32 -> 47, of which waited for: 32 -> 40; matrix products, arithmetic and copies ran while one was open for 0% -> 0% of each run, Pallas kernels for 0% -> 0%
where the time goes in v1:
time: 506 us; the launch traced here: 504 us
  waiting for transfers between devices  381 us (75%)
  starting transfers between devices  81.4 us (16%)
  blocking collectives  14.5 us (3%)
  between operations  14.2 us (3%)
  matrix products  10.7 us (2%)
    ppermute x31, waiting for transfers between devices, passed_along(): return lax.ppermute(x, axis, pairs)  317 us
    ppermute x31, starting transfers between devices, passed_along(): return lax.ppermute(x, axis, pairs)  60.6 us
    all_gather x1, waiting for transfers between devices, body(): lax.all_gather(picked_one, 'blk', axis=0, tiled=True)  46.4 us
    ppermute x7, starting transfers between devices, collect(): lax.ppermute(going_down, axis, [(d, (d - 1) % ways) for d in range(ways)])  20.4 us
    ppermute x8, waiting for transfers between devices, collect(): lax.ppermute(going_up, axis, [(d, (d + 1) % ways) for d in range(ways)])  17.6 us
    all_gather x1, blocking collectives, body(): lax.all_gather(edge_rows, 'blk', axis=0, tiled=True).astype(jnp.float32)  14.5 us
  transfers between devices with their start and end apart: 47, of which 40 were waited for; matrix products, arithmetic and copies ran while one was open for 0% of the time, Pallas kernels for 0%

profile of v1, /device:TPU:32, one launch (start us, length us, event | category | flops | bytes accessed | tf_op | source)
XLA Modules:
  0.0 504.5 jit_solution(7437881353997894525)
XLA Ops:
  8.1 2.6 convolution_convert_fusion.1
  10.7 46.4 %all-gather.2.cloned.1.call-done = bf16[256,2048]{1,0:T(8,128)(2,1)} async-done(((bf16[16,2048]{1,0:T(8,128)(2,1)}), bf16[256,2048]{1,0:T(8,128)(2,1)}) %all-gather.2.cloned.1.call-update) | async-done | bytes 1048592 | tf_op jit(solution)/shard_map/all_gather | solution.py:62
  57.1 2.8 subtract_convert_fusion
  60.7 2.7 collective-permute-start.2
  65.2 3.0 collective-permute-start.4
  70.1 3.0 collective-permute-start.6
  74.9 3.0 collective-permute-start.8
  79.7 3.0 collective-permute-start.10
  84.5 3.0 collective-permute-start.12
  89.3 3.0 collective-permute-start.14
  94.2 4.8 collective-permute-done.15
  99.0 3.0 subtract_convert_fusion.1
  103.1 14.5 %all_gather.7 = bf16[256,256]{1,0:T(8,128)(2,1)S(1)} all-gather(bf16[16,256]{1,0:T(8,128)(2,1)S(1)} %convolution_convert_fusion.4), channel_id=1, replica_groups=mesh['tm'=32,'blk'=16] {'blk'}, dimensions={0}, use_global_device_ids=true | all-gather | bytes 139264 | tf_op jit(solution)/shard_map/all_gather | solution.py:80
  117.6 379.3 %while.16 = (s32[]{:T(128)}, f32[256,256]{1,0:T(8,128)S(1)}, s32[]{:T(128)}, f32[256,256]{1,0:T(8,128)S(1)}, f32[256,256]{1,0:T(8,128)S(1)}, /*index=5*/s32[]{:T(128)}) while((s32[]{:T(128)}, f32[256,256]{1,0:T(8,128)S(1)}, s32[]{:T(128)}, f32[256,256]{1,0:T(8,128)S(1)}, f32[256,256]{1,0:T(8,128)S(1)}, /*index=5*/s32[]{:T(128)}) %tuple.52), condition=%wide.region_3.4_spmd, body=%wide.region_0.3_spmd.sunk | while | flops 402718720 | bytes 2883739 | solution.py:96
  117.6 3.4 collective-permute-start
  121.0 10.4 %collective-permute-done = f32[256,256]{1,0:T(8,128)S(1)} collective-permute-done((f32[256,256]{1,0:T(8,128)S(1)}, f32[256,256]{1,0:T(8,128)S(1)}, u32[]{:S(2)}, u32[]{:S(2)}) %collective-permute-start) | collective-permute-done | bytes 262176 | tf_op jit(solution)/shard_map/while/body/eval_jaxpr/ppermute | solution.py:28
  131.4 1.9 collective-permute-start
  133.3 11.0 %collective-permute-done = f32[256,256]{1,0:T(8,128)S(1)} collective-permute-done((f32[256,256]{1,0:T(8,128)S(1)}, f32[256,256]{1,0:T(8,128)S(1)}, u32[]{:S(2)}, u32[]{:S(2)}) %collective-permute-start) | collective-permute-done | bytes 262176 | tf_op jit(solution)/shard_map/while/body/eval_jaxpr/ppermute | solution.py:28
  144.3 1.9 collective-permute-start
  146.3 10.1 %collective-permute-done = f32[256,256]{1,0:T(8,128)S(1)} collective-permute-done((f32[256,256]{1,0:T(8,128)S(1)}, f32[256,256]{1,0:T(8,128)S(1)}, u32[]{:S(2)}, u32[]{:S(2)}) %collective-permute-start) | collective-permute-done | bytes 262176 | tf_op jit(solution)/shard_map/while/body/eval_jaxpr/ppermute | solution.py:28
  156.4 1.9 collective-permute-start
  158.3 9.7 %collective-permute-done = f32[256,256]{1,0:T(8,128)S(1)} collective-permute-done((f32[256,256]{1,0:T(8,128)S(1)}, f32[256,256]{1,0:T(8,128)S(1)}, u32[]{:S(2)}, u32[]{:S(2)}) %collective-permute-start) | collective-permute-done | bytes 262176 | tf_op jit(solution)/shard_map/while/body/eval_jaxpr/ppermute | solution.py:28
  168.0 1.9 collective-permute-start
  169.9 9.7 %collective-permute-done = f32[256,256]{1,0:T(8,128)S(1)} collective-permute-done((f32[256,256]{1,0:T(8,128)S(1)}, f32[256,256]{1,0:T(8,128)S(1)}, u32[]{:S(2)}, u32[]{:S(2)}) %collective-permute-start) | collective-permute-done | bytes 262176 | tf_op jit(solution)/shard_map/while/body/eval_jaxpr/ppermute | solution.py:28
  179.5 1.9 collective-permute-start
  181.5 9.7 %collective-permute-done = f32[256,256]{1,0:T(8,128)S(1)} collective-permute-done((f32[256,256]{1,0:T(8,128)S(1)}, f32[256,256]{1,0:T(8,128)S(1)}, u32[]{:S(2)}, u32[]{:S(2)}) %collective-permute-start) | collective-permute-done | bytes 262176 | tf_op jit(solution)/shard_map/while/body/eval_jaxpr/ppermute | solution.py:28
  191.1 1.9 collective-permute-start
  193.0 9.7 %collective-permute-done = f32[256,256]{1,0:T(8,128)S(1)} collective-permute-done((f32[256,256]{1,0:T(8,128)S(1)}, f32[256,256]{1,0:T(8,128)S(1)}, u32[]{:S(2)}, u32[]{:S(2)}) %collective-permute-start) | collective-permute-done | bytes 262176 | tf_op jit(solution)/shard_map/while/body/eval_jaxpr/ppermute | solution.py:28
  202.7 1.9 collective-permute-start
  204.6 9.8 %collective-permute-done = f32[256,256]{1,0:T(8,128)S(1)} collective-permute-done((f32[256,256]{1,0:T(8,128)S(1)}, f32[256,256]{1,0:T(8,128)S(1)}, u32[]{:S(2)}, u32[]{:S(2)}) %collective-permute-start) | collective-permute-done | bytes 262176 | tf_op jit(solution)/shard_map/while/body/eval_jaxpr/ppermute | solution.py:28
  214.4 1.9 collective-permute-start
  216.4 10.9 %collective-permute-done = f32[256,256]{1,0:T(8,128)S(1)} collective-permute-done((f32[256,256]{1,0:T(8,128)S(1)}, f32[256,256]{1,0:T(8,128)S(1)}, u32[]{:S(2)}, u32[]{:S(2)}) %collective-permute-start) | collective-permute-done | bytes 262176 | tf_op jit(solution)/shard_map/while/body/eval_jaxpr/ppermute | solution.py:28
  227.3 1.9 collective-permute-start
  229.2 12.1 %collective-permute-done = f32[256,256]{1,0:T(8,128)S(1)} collective-permute-done((f32[256,256]{1,0:T(8,128)S(1)}, f32[256,256]{1,0:T(8,128)S(1)}, u32[]{:S(2)}, u32[]{:S(2)}) %collective-permute-start) | collective-permute-done | bytes 262176 | tf_op jit(solution)/shard_map/while/body/eval_jaxpr/ppermute | solution.py:28
  241.3 1.9 collective-permute-start
  243.3 11.6 %collective-permute-done = f32[256,256]{1,0:T(8,128)S(1)} collective-permute-done((f32[256,256]{1,0:T(8,128)S(1)}, f32[256,256]{1,0:T(8,128)S(1)}, u32[]{:S(2)}, u32[]{:S(2)}) %collective-permute-start) | collective-permute-done | bytes 262176 | tf_op jit(solution)/shard_map/while/body/eval_jaxpr/ppermute | solution.py:28
  254.9 1.9 collective-permute-start
  256.8 10.8 %collective-permute-done = f32[256,256]{1,0:T(8,128)S(1)} collective-permute-done((f32[256,256]{1,0:T(8,128)S(1)}, f32[256,256]{1,0:T(8,128)S(1)}, u32[]{:S(2)}, u32[]{:S(2)}) %collective-permute-start) | collective-permute-done | bytes 262176 | tf_op jit(solution)/shard_map/while/body/eval_jaxpr/ppermute | solution.py:28
  267.6 1.9 collective-permute-start
  269.5 9.9 %collective-permute-done = f32[256,256]{1,0:T(8,128)S(1)} collective-permute-done((f32[256,256]{1,0:T(8,128)S(1)}, f32[256,256]{1,0:T(8,128)S(1)}, u32[]{:S(2)}, u32[]{:S(2)}) %collective-permute-start) | collective-permute-done | bytes 262176 | tf_op jit(solution)/shard_map/while/body/eval_jaxpr/ppermute | solution.py:28
  279.4 1.9 collective-permute-start
  281.3 9.7 %collective-permute-done = f32[256,256]{1,0:T(8,128)S(1)} collective-permute-done((f32[256,256]{1,0:T(8,128)S(1)}, f32[256,256]{1,0:T(8,128)S(1)}, u32[]{:S(2)}, u32[]{:S(2)}) %collective-permute-start) | collective-permute-done | bytes 262176 | tf_op jit(solution)/shard_map/while/body/eval_jaxpr/ppermute | solution.py:28
  291.0 1.9 collective-permute-start
  292.9 9.7 %collective-permute-done = f32[256,256]{1,0:T(8,128)S(1)} collective-permute-done((f32[256,256]{1,0:T(8,128)S(1)}, f32[256,256]{1,0:T(8,128)S(1)}, u32[]{:S(2)}, u32[]{:S(2)}) %collective-permute-start) | collective-permute-done | bytes 262176 | tf_op jit(solution)/shard_map/while/body/eval_jaxpr/ppermute | solution.py:28
  302.6 1.9 collective-permute-start
  304.5 9.7 %collective-permute-done = f32[256,256]{1,0:T(8,128)S(1)} collective-permute-done((f32[256,256]{1,0:T(8,128)S(1)}, f32[256,256]{1,0:T(8,128)S(1)}, u32[]{:S(2)}, u32[]{:S(2)}) %collective-permute-start) | collective-permute-done | bytes 262176 | tf_op jit(solution)/shard_map/while/body/eval_jaxpr/ppermute | solution.py:28
  314.9 1.9 collective-permute-start
  316.9 9.7 %collective-permute-done = f32[256,256]{1,0:T(8,128)S(1)} collective-permute-done((f32[256,256]{1,0:T(8,128)S(1)}, f32[256,256]{1,0:T(8,128)S(1)}, u32[]{:S(2)}, u32[]{:S(2)}) %collective-permute-start) | collective-permute-done | bytes 262176 | tf_op jit(solution)/shard_map/while/body/eval_jaxpr/ppermute | solution.py:28
  328.5 10.1 %collective-permute-done = f32[256,256]{1,0:T(8,128)S(1)} collective-permute-done((f32[256,256]{1,0:T(8,128)S(1)}, f32[256,256]{1,0:T(8,128)S(1)}, u32[]{:S(2)}, u32[]{:S(2)}) %collective-permute-start) | collective-permute-done | bytes 262176 | tf_op jit(solution)/shard_map/while/body/eval_jaxpr/ppermute | solution.py:28
  340.5 11.2 %collective-permute-done = f32[256,256]{1,0:T(8,128)S(1)} collective-permute-done((f32[256,256]{1,0:T(8,128)S(1)}, f32[256,256]{1,0:T(8,128)S(1)}, u32[]{:S(2)}, u32[]{:S(2)}) %collective-permute-start) | collective-permute-done | bytes 262176 | tf_op jit(solution)/shard_map/while/body/eval_jaxpr/ppermute | solution.py:28
  353.6 12.3 %collective-permute-done = f32[256,256]{1,0:T(8,128)S(1)} collective-permute-done((f32[256,256]{1,0:T(8,128)S(1)}, f32[256,256]{1,0:T(8,128)S(1)}, u32[]{:S(2)}, u32[]{:S(2)}) %collective-permute-start) | collective-permute-done | bytes 262176 | tf_op jit(solution)/shard_map/while/body/eval_jaxpr/ppermute | solution.py:28
  367.8 11.6 %collective-permute-done = f32[256,256]{1,0:T(8,128)S(1)} collective-permute-done((f32[256,256]{1,0:T(8,128)S(1)}, f32[256,256]{1,0:T(8,128)S(1)}, u32[]{:S(2)}, u32[]{:S(2)}) %collective-permute-start) | collective-permute-done | bytes 262176 | tf_op jit(solution)/shard_map/while/body/eval_jaxpr/ppermute | solution.py:28
  379.4 1.9 collective-permute-start
  381.4 10.8 %collective-permute-done = f32[256,256]{1,0:T(8,128)S(1)} collective-permute-done((f32[256,256]{1,0:T(8,128)S(1)}, f32[256,256]{1,0:T(8,128)S(1)}, u32[]{:S(2)}, u32[]{:S(2)}) %collective-permute-start) | collective-permute-done | bytes 262176 | tf_op jit(solution)/shard_map/while/body/eval_jaxpr/ppermute | solution.py:28
  394.1 9.8 %collective-permute-done = f32[256,256]{1,0:T(8,128)S(1)} collective-permute-done((f32[256,256]{1,0:T(8,128)S(1)}, f32[256,256]{1,0:T(8,128)S(1)}, u32[]{:S(2)}, u32[]{:S(2)}) %collective-permute-start) | collective-permute-done | bytes 262176 | tf_op jit(solution)/shard_map/while/body/eval_jaxpr/ppermute | solution.py:28
  403.9 1.9 collective-permute-start
  405.8 9.7 %collective-permute-done = f32[256,256]{1,0:T(8,128)S(1)} collective-permute-done((f32[256,256]{1,0:T(8,128)S(1)}, f32[256,256]{1,0:T(8,128)S(1)}, u32[]{:S(2)}, u32[]{:S(2)}) %collective-permute-start) | collective-permute-done | bytes 262176 | tf_op jit(solution)/shard_map/while/body/eval_jaxpr/ppermute | solution.py:28
  417.4 9.7 %collective-permute-done = f32[256,256]{1,0:T(8,128)S(1)} collective-permute-done((f32[256,256]{1,0:T(8,128)S(1)}, f32[256,256]{1,0:T(8,128)S(1)}, u32[]{:S(2)}, u32[]{:S(2)}) %collective-permute-start) | collective-permute-done | bytes 262176 | tf_op jit(solution)/shard_map/while/body/eval_jaxpr/ppermute | solution.py:28
  429.0 9.7 %collective-permute-done = f32[256,256]{1,0:T(8,128)S(1)} collective-permute-done((f32[256,256]{1,0:T(8,128)S(1)}, f32[256,256]{1,0:T(8,128)S(1)}, u32[]{:S(2)}, u32[]{:S(2)}) %collective-permute-start) | collective-permute-done | bytes 262176 | tf_op jit(solution)/shard_map/while/body/eval_jaxpr/ppermute | solution.py:28
  440.6 9.7 %collective-permute-done = f32[256,256]{1,0:T(8,128)S(1)} collective-permute-done((f32[256,256]{1,0:T(8,128)S(1)}, f32[256,256]{1,0:T(8,128)S(1)}, u32[]{:S(2)}, u32[]{:S(2)}) %collective-permute-start) | collective-permute-done | bytes 262176 | tf_op jit(solution)/shard_map/while/body/eval_jaxpr/ppermute | solution.py:28
  452.1 10.1 %collective-permute-done = f32[256,256]{1,0:T(8,128)S(1)} collective-permute-done((f32[256,256]{1,0:T(8,128)S(1)}, f32[256,256]{1,0:T(8,128)S(1)}, u32[]{:S(2)}, u32[]{:S(2)}) %collective-permute-start) | collective-permute-done | bytes 262176 | tf_op jit(solution)/shard_map/while/body/eval_jaxpr/ppermute | solution.py:28
  464.1 9.7 %collective-permute-done = f32[256,256]{1,0:T(8,128)S(1)} collective-permute-done((f32[256,256]{1,0:T(8,128)S(1)}, f32[256,256]{1,0:T(8,128)S(1)}, u32[]{:S(2)}, u32[]{:S(2)}) %collective-permute-start) | collective-permute-done | bytes 262176 | tf_op jit(solution)/shard_map/while/body/eval_jaxpr/ppermute | solution.py:28
  475.7 9.7 %collective-permute-done = f32[256,256]{1,0:T(8,128)S(1)} collective-permute-done((f32[256,256]{1,0:T(8,128)S(1)}, f32[256,256]{1,0:T(8,128)S(1)}, u32[]{:S(2)}, u32[]{:S(2)}) %collective-permute-start) | collective-permute-done | bytes 262176 | tf_op jit(solution)/shard_map/while/body/eval_jaxpr/ppermute | solution.py:28
  487.3 9.7 %collective-permute-done = f32[256,256]{1,0:T(8,128)S(1)} collective-permute-done((f32[256,256]{1,0:T(8,128)S(1)}, f32[256,256]{1,0:T(8,128)S(1)}, u32[]{:S(2)}, u32[]{:S(2)}) %collective-permute-start) | collective-permute-done | bytes 262176 | tf_op jit(solution)/shard_map/while/body/eval_jaxpr/ppermute | solution.py:28
  (97 shorter events, 41.0 us)
Async XLA Ops:
  7.2 50.0 %copy-start.2 = (bf16[1,2,256,256]{3,2,1,0:T(8,128)(2,1)S(1)}, bf16[1,2,256,256]{3,2,1,0:T(8,128)(2,1)}, u32[]{:S(2)}) copy-start(bf16[1,2,256,256]{3,2,1,0:T(8,128)(2,1)} %param.9) | copy-start | bytes 786436
  7.2 50.0 %all-gather.2.cloned.1.call-start = ((), (), s32[]{:S(2)}) async-start(), calls=%async_computation | async-start | bytes 1114112 | tf_op jit(solution)/shard_map/all_gather | solution.py:62
  60.4 4.8 collective-permute-start.1
  60.7 4.6 collective-permute-start.2
  65.2 4.8 collective-permute-start.3
  65.2 4.8 collective-permute-start.4
  70.1 4.8 collective-permute-start.5
  70.1 4.8 collective-permute-start.6
  74.9 4.8 collective-permute-start.7
  74.9 4.8 collective-permute-start.8
  79.7 4.8 collective-permute-start.9
  79.7 4.8 collective-permute-start.10
  84.5 4.8 collective-permute-start.11
  84.5 4.8 collective-permute-start.12
  89.3 4.8 collective-permute-start.13
  89.3 4.8 collective-permute-start.14
  94.1 4.8 collective-permute-start.15
  98.9 18.7 %copy-start = (f32[1,256,256]{2,1,0:T(8,128)S(1)}, f32[1,256,256]{2,1,0:T(8,128)}, u32[]{:S(2)}) copy-start(f32[1,256,256]{2,1,0:T(8,128)} %param.10) | copy-start | bytes 786436
  117.6 13.8 %collective-permute-start = (f32[256,256]{1,0:T(8,128)S(1)}, f32[256,256]{1,0:T(8,128)S(1)}, u32[]{:S(2)}, u32[]{:S(2)}) collective-permute-start(f32[256,256]{1,0:T(8,128)S(1)} %get-tuple-element.164), channel_id=1, source_target_pairs={{0,16},{16,32},{32,48},{48,64},{64,80},{80,96},{96,112},{112,128},... | collective-permute-start | bytes 786440 | tf_op jit(solution)/shard_map/while/body/eval_jaxpr/ppermute | solution.py:28
  131.4 13.0 %collective-permute-start = (f32[256,256]{1,0:T(8,128)S(1)}, f32[256,256]{1,0:T(8,128)S(1)}, u32[]{:S(2)}, u32[]{:S(2)}) collective-permute-start(f32[256,256]{1,0:T(8,128)S(1)} %get-tuple-element.164), channel_id=1, source_target_pairs={{0,16},{16,32},{32,48},{48,64},{64,80},{80,96},{96,112},{112,128},... | collective-permute-start | bytes 786440 | tf_op jit(solution)/shard_map/while/body/eval_jaxpr/ppermute | solution.py:28
  144.3 12.0 %collective-permute-start = (f32[256,256]{1,0:T(8,128)S(1)}, f32[256,256]{1,0:T(8,128)S(1)}, u32[]{:S(2)}, u32[]{:S(2)}) collective-permute-start(f32[256,256]{1,0:T(8,128)S(1)} %get-tuple-element.164), channel_id=1, source_target_pairs={{0,16},{16,32},{32,48},{48,64},{64,80},{80,96},{96,112},{112,128},... | collective-permute-start | bytes 786440 | tf_op jit(solution)/shard_map/while/body/eval_jaxpr/ppermute | solution.py:28
  156.4 11.6 %collective-permute-start = (f32[256,256]{1,0:T(8,128)S(1)}, f32[256,256]{1,0:T(8,128)S(1)}, u32[]{:S(2)}, u32[]{:S(2)}) collective-permute-start(f32[256,256]{1,0:T(8,128)S(1)} %get-tuple-element.164), channel_id=1, source_target_pairs={{0,16},{16,32},{32,48},{48,64},{64,80},{80,96},{96,112},{112,128},... | collective-permute-start | bytes 786440 | tf_op jit(solution)/shard_map/while/body/eval_jaxpr/ppermute | solution.py:28
  168.0 11.6 %collective-permute-start = (f32[256,256]{1,0:T(8,128)S(1)}, f32[256,256]{1,0:T(8,128)S(1)}, u32[]{:S(2)}, u32[]{:S(2)}) collective-permute-start(f32[256,256]{1,0:T(8,128)S(1)} %get-tuple-element.164), channel_id=1, source_target_pairs={{0,16},{16,32},{32,48},{48,64},{64,80},{80,96},{96,112},{112,128},... | collective-permute-start | bytes 786440 | tf_op jit(solution)/shard_map/while/body/eval_jaxpr/ppermute | solution.py:28
  179.5 11.6 %collective-permute-start = (f32[256,256]{1,0:T(8,128)S(1)}, f32[256,256]{1,0:T(8,128)S(1)}, u32[]{:S(2)}, u32[]{:S(2)}) collective-permute-start(f32[256,256]{1,0:T(8,128)S(1)} %get-tuple-element.164), channel_id=1, source_target_pairs={{0,16},{16,32},{32,48},{48,64},{64,80},{80,96},{96,112},{112,128},... | collective-permute-start | bytes 786440 | tf_op jit(solution)/shard_map/while/body/eval_jaxpr/ppermute | solution.py:28
  191.1 11.6 %collective-permute-start = (f32[256,256]{1,0:T(8,128)S(1)}, f32[256,256]{1,0:T(8,128)S(1)}, u32[]{:S(2)}, u32[]{:S(2)}) collective-permute-start(f32[256,256]{1,0:T(8,128)S(1)} %get-tuple-element.164), channel_id=1, source_target_pairs={{0,16},{16,32},{32,48},{48,64},{64,80},{80,96},{96,112},{112,128},... | collective-permute-start | bytes 786440 | tf_op jit(solution)/shard_map/while/body/eval_jaxpr/ppermute | solution.py:28
  202.7 11.8 %collective-permute-start = (f32[256,256]{1,0:T(8,128)S(1)}, f32[256,256]{1,0:T(8,128)S(1)}, u32[]{:S(2)}, u32[]{:S(2)}) collective-permute-start(f32[256,256]{1,0:T(8,128)S(1)} %get-tuple-element.164), channel_id=1, source_target_pairs={{0,16},{16,32},{32,48},{48,64},{64,80},{80,96},{96,112},{112,128},... | collective-permute-start | bytes 786440 | tf_op jit(solution)/shard_map/while/body/eval_jaxpr/ppermute | solution.py:28
  214.4 12.8 %collective-permute-start = (f32[256,256]{1,0:T(8,128)S(1)}, f32[256,256]{1,0:T(8,128)S(1)}, u32[]{:S(2)}, u32[]{:S(2)}) collective-permute-start(f32[256,256]{1,0:T(8,128)S(1)} %get-tuple-element.164), channel_id=1, source_target_pairs={{0,16},{16,32},{32,48},{48,64},{64,80},{80,96},{96,112},{112,128},... | collective-permute-start | bytes 786440 | tf_op jit(solution)/shard_map/while/body/eval_jaxpr/ppermute | solution.py:28
  227.3 14.1 %collective-permute-start = (f32[256,256]{1,0:T(8,128)S(1)}, f32[256,256]{1,0:T(8,128)S(1)}, u32[]{:S(2)}, u32[]{:S(2)}) collective-permute-start(f32[256,256]{1,0:T(8,128)S(1)} %get-tuple-element.164), channel_id=1, source_target_pairs={{0,16},{16,32},{32,48},{48,64},{64,80},{80,96},{96,112},{112,128},... | collective-permute-start | bytes 786440 | tf_op jit(solution)/shard_map/while/body/eval_jaxpr/ppermute | solution.py:28
  241.3 13.5 %collective-permute-start = (f32[256,256]{1,0:T(8,128)S(1)}, f32[256,256]{1,0:T(8,128)S(1)}, u32[]{:S(2)}, u32[]{:S(2)}) collective-permute-start(f32[256,256]{1,0:T(8,128)S(1)} %get-tuple-element.164), channel_id=1, source_target_pairs={{0,16},{16,32},{32,48},{48,64},{64,80},{80,96},{96,112},{112,128},... | collective-permute-start | bytes 786440 | tf_op jit(solution)/shard_map/while/body/eval_jaxpr/ppermute | solution.py:28
  254.9 12.7 %collective-permute-start = (f32[256,256]{1,0:T(8,128)S(1)}, f32[256,256]{1,0:T(8,128)S(1)}, u32[]{:S(2)}, u32[]{:S(2)}) collective-permute-start(f32[256,256]{1,0:T(8,128)S(1)} %get-tuple-element.164), channel_id=1, source_target_pairs={{0,16},{16,32},{32,48},{48,64},{64,80},{80,96},{96,112},{112,128},... | collective-permute-start | bytes 786440 | tf_op jit(solution)/shard_map/while/body/eval_jaxpr/ppermute | solution.py:28
  267.6 11.8 %collective-permute-start = (f32[256,256]{1,0:T(8,128)S(1)}, f32[256,256]{1,0:T(8,128)S(1)}, u32[]{:S(2)}, u32[]{:S(2)}) collective-permute-start(f32[256,256]{1,0:T(8,128)S(1)} %get-tuple-element.164), channel_id=1, source_target_pairs={{0,16},{16,32},{32,48},{48,64},{64,80},{80,96},{96,112},{112,128},... | collective-permute-start | bytes 786440 | tf_op jit(solution)/shard_map/while/body/eval_jaxpr/ppermute | solution.py:28
  279.4 11.6 %collective-permute-start = (f32[256,256]{1,0:T(8,128)S(1)}, f32[256,256]{1,0:T(8,128)S(1)}, u32[]{:S(2)}, u32[]{:S(2)}) collective-permute-start(f32[256,256]{1,0:T(8,128)S(1)} %get-tuple-element.164), channel_id=1, source_target_pairs={{0,16},{16,32},{32,48},{48,64},{64,80},{80,96},{96,112},{112,128},... | collective-permute-start | bytes 786440 | tf_op jit(solution)/shard_map/while/body/eval_jaxpr/ppermute | solution.py:28
  291.0 11.6 %collective-permute-start = (f32[256,256]{1,0:T(8,128)S(1)}, f32[256,256]{1,0:T(8,128)S(1)}, u32[]{:S(2)}, u32[]{:S(2)}) collective-permute-start(f32[256,256]{1,0:T(8,128)S(1)} %get-tuple-element.164), channel_id=1, source_target_pairs={{0,16},{16,32},{32,48},{48,64},{64,80},{80,96},{96,112},{112,128},... | collective-permute-start | bytes 786440 | tf_op jit(solution)/shard_map/while/body/eval_jaxpr/ppermute | solution.py:28
  302.6 11.6 %collective-permute-start = (f32[256,256]{1,0:T(8,128)S(1)}, f32[256,256]{1,0:T(8,128)S(1)}, u32[]{:S(2)}, u32[]{:S(2)}) collective-permute-start(f32[256,256]{1,0:T(8,128)S(1)} %get-tuple-element.164), channel_id=1, source_target_pairs={{0,16},{16,32},{32,48},{48,64},{64,80},{80,96},{96,112},{112,128},... | collective-permute-start | bytes 786440 | tf_op jit(solution)/shard_map/while/body/eval_jaxpr/ppermute | solution.py:28
  314.9 11.6 %collective-permute-start = (f32[256,256]{1,0:T(8,128)S(1)}, f32[256,256]{1,0:T(8,128)S(1)}, u32[]{:S(2)}, u32[]{:S(2)}) collective-permute-start(f32[256,256]{1,0:T(8,128)S(1)} %get-tuple-element.164), channel_id=1, source_target_pairs={{0,16},{16,32},{32,48},{48,64},{64,80},{80,96},{96,112},{112,128},... | collective-permute-start | bytes 786440 | tf_op jit(solution)/shard_map/while/body/eval_jaxpr/ppermute | solution.py:28
  326.5 12.0 %collective-permute-start = (f32[256,256]{1,0:T(8,128)S(1)}, f32[256,256]{1,0:T(8,128)S(1)}, u32[]{:S(2)}, u32[]{:S(2)}) collective-permute-start(f32[256,256]{1,0:T(8,128)S(1)} %get-tuple-element.164), channel_id=1, source_target_pairs={{0,16},{16,32},{32,48},{48,64},{64,80},{80,96},{96,112},{112,128},... | collective-permute-start | bytes 786440 | tf_op jit(solution)/shard_map/while/body/eval_jaxpr/ppermute | solution.py:28
  338.5 13.1 %collective-permute-start = (f32[256,256]{1,0:T(8,128)S(1)}, f32[256,256]{1,0:T(8,128)S(1)}, u32[]{:S(2)}, u32[]{:S(2)}) collective-permute-start(f32[256,256]{1,0:T(8,128)S(1)} %get-tuple-element.164), channel_id=1, source_target_pairs={{0,16},{16,32},{32,48},{48,64},{64,80},{80,96},{96,112},{112,128},... | collective-permute-start | bytes 786440 | tf_op jit(solution)/shard_map/while/body/eval_jaxpr/ppermute | solution.py:28
  351.6 14.3 %collective-permute-start = (f32[256,256]{1,0:T(8,128)S(1)}, f32[256,256]{1,0:T(8,128)S(1)}, u32[]{:S(2)}, u32[]{:S(2)}) collective-permute-start(f32[256,256]{1,0:T(8,128)S(1)} %get-tuple-element.164), channel_id=1, source_target_pairs={{0,16},{16,32},{32,48},{48,64},{64,80},{80,96},{96,112},{112,128},... | collective-permute-start | bytes 786440 | tf_op jit(solution)/shard_map/while/body/eval_jaxpr/ppermute | solution.py:28
  365.9 13.5 %collective-permute-start = (f32[256,256]{1,0:T(8,128)S(1)}, f32[256,256]{1,0:T(8,128)S(1)}, u32[]{:S(2)}, u32[]{:S(2)}) collective-permute-start(f32[256,256]{1,0:T(8,128)S(1)} %get-tuple-element.164), channel_id=1, source_target_pairs={{0,16},{16,32},{32,48},{48,64},{64,80},{80,96},{96,112},{112,128},... | collective-permute-start | bytes 786440 | tf_op jit(solution)/shard_map/while/body/eval_jaxpr/ppermute | solution.py:28
  379.4 12.7 %collective-permute-start = (f32[256,256]{1,0:T(8,128)S(1)}, f32[256,256]{1,0:T(8,128)S(1)}, u32[]{:S(2)}, u32[]{:S(2)}) collective-permute-start(f32[256,256]{1,0:T(8,128)S(1)} %get-tuple-element.164), channel_id=1, source_target_pairs={{0,16},{16,32},{32,48},{48,64},{64,80},{80,96},{96,112},{112,128},... | collective-permute-start | bytes 786440 | tf_op jit(solution)/shard_map/while/body/eval_jaxpr/ppermute | solution.py:28
  392.1 11.8 %collective-permute-start = (f32[256,256]{1,0:T(8,128)S(1)}, f32[256,256]{1,0:T(8,128)S(1)}, u32[]{:S(2)}, u32[]{:S(2)}) collective-permute-start(f32[256,256]{1,0:T(8,128)S(1)} %get-tuple-element.164), channel_id=1, source_target_pairs={{0,16},{16,32},{32,48},{48,64},{64,80},{80,96},{96,112},{112,128},... | collective-permute-start | bytes 786440 | tf_op jit(solution)/shard_map/while/body/eval_jaxpr/ppermute | solution.py:28
  403.9 11.6 %collective-permute-start = (f32[256,256]{1,0:T(8,128)S(1)}, f32[256,256]{1,0:T(8,128)S(1)}, u32[]{:S(2)}, u32[]{:S(2)}) collective-permute-start(f32[256,256]{1,0:T(8,128)S(1)} %get-tuple-element.164), channel_id=1, source_target_pairs={{0,16},{16,32},{32,48},{48,64},{64,80},{80,96},{96,112},{112,128},... | collective-permute-start | bytes 786440 | tf_op jit(solution)/shard_map/while/body/eval_jaxpr/ppermute | solution.py:28
  415.5 11.6 %collective-permute-start = (f32[256,256]{1,0:T(8,128)S(1)}, f32[256,256]{1,0:T(8,128)S(1)}, u32[]{:S(2)}, u32[]{:S(2)}) collective-permute-start(f32[256,256]{1,0:T(8,128)S(1)} %get-tuple-element.164), channel_id=1, source_target_pairs={{0,16},{16,32},{32,48},{48,64},{64,80},{80,96},{96,112},{112,128},... | collective-permute-start | bytes 786440 | tf_op jit(solution)/shard_map/while/body/eval_jaxpr/ppermute | solution.py:28
  427.1 11.6 %collective-permute-start = (f32[256,256]{1,0:T(8,128)S(1)}, f32[256,256]{1,0:T(8,128)S(1)}, u32[]{:S(2)}, u32[]{:S(2)}) collective-permute-start(f32[256,256]{1,0:T(8,128)S(1)} %get-tuple-element.164), channel_id=1, source_target_pairs={{0,16},{16,32},{32,48},{48,64},{64,80},{80,96},{96,112},{112,128},... | collective-permute-start | bytes 786440 | tf_op jit(solution)/shard_map/while/body/eval_jaxpr/ppermute | solution.py:28
  438.6 11.6 %collective-permute-start = (f32[256,256]{1,0:T(8,128)S(1)}, f32[256,256]{1,0:T(8,128)S(1)}, u32[]{:S(2)}, u32[]{:S(2)}) collective-permute-start(f32[256,256]{1,0:T(8,128)S(1)} %get-tuple-element.164), channel_id=1, source_target_pairs={{0,16},{16,32},{32,48},{48,64},{64,80},{80,96},{96,112},{112,128},... | collective-permute-start | bytes 786440 | tf_op jit(solution)/shard_map/while/body/eval_jaxpr/ppermute | solution.py:28
  450.2 12.0 %collective-permute-start = (f32[256,256]{1,0:T(8,128)S(1)}, f32[256,256]{1,0:T(8,128)S(1)}, u32[]{:S(2)}, u32[]{:S(2)}) collective-permute-start(f32[256,256]{1,0:T(8,128)S(1)} %get-tuple-element.164), channel_id=1, source_target_pairs={{0,16},{16,32},{32,48},{48,64},{64,80},{80,96},{96,112},{112,128},... | collective-permute-start | bytes 786440 | tf_op jit(solution)/shard_map/while/body/eval_jaxpr/ppermute | solution.py:28
  462.2 11.6 %collective-permute-start = (f32[256,256]{1,0:T(8,128)S(1)}, f32[256,256]{1,0:T(8,128)S(1)}, u32[]{:S(2)}, u32[]{:S(2)}) collective-permute-start(f32[256,256]{1,0:T(8,128)S(1)} %get-tuple-element.164), channel_id=1, source_target_pairs={{0,16},{16,32},{32,48},{48,64},{64,80},{80,96},{96,112},{112,128},... | collective-permute-start | bytes 786440 | tf_op jit(solution)/shard_map/while/body/eval_jaxpr/ppermute | solution.py:28
  473.8 11.6 %collective-permute-start = (f32[256,256]{1,0:T(8,128)S(1)}, f32[256,256]{1,0:T(8,128)S(1)}, u32[]{:S(2)}, u32[]{:S(2)}) collective-permute-start(f32[256,256]{1,0:T(8,128)S(1)} %get-tuple-element.164), channel_id=1, source_target_pairs={{0,16},{16,32},{32,48},{48,64},{64,80},{80,96},{96,112},{112,128},... | collective-permute-start | bytes 786440 | tf_op jit(solution)/shard_map/while/body/eval_jaxpr/ppermute | solution.py:28
  485.4 11.6 %collective-permute-start = (f32[256,256]{1,0:T(8,128)S(1)}, f32[256,256]{1,0:T(8,128)S(1)}, u32[]{:S(2)}, u32[]{:S(2)}) collective-permute-start(f32[256,256]{1,0:T(8,128)S(1)} %get-tuple-element.164), channel_id=1, source_target_pairs={{0,16},{16,32},{32,48},{48,64},{64,80},{80,96},{96,112},{112,128},... | collective-permute-start | bytes 786440 | tf_op jit(solution)/shard_map/while/body/eval_jaxpr/ppermute | solution.py:28
  496.9 0.7 copy-start.1
Sparse Core Ops, SparseCore 0:
  10.9 46.2 all-gather.1
